TPU v7x, 256 devices: a whole 4x4x8 slice. The times are simulated.
256 devices in a mesh: expert: 64 (over z, y, core), dp: 4 (over x).
Axes of the slice: x: 4, y: 4, z: 8, core: 2. Of those that a mesh axis runs over, the one named last changes fastest.
Arguments:
- prenorm_input: bfloat16 [32768, 1280], P(('expert', 'dp')), may hold values from -6 to 6
- gain: float32 [1280], replicated, may hold values from 0.25 to 1.75
- router: bfloat16 [1280, 32], replicated, may hold values from -0.15625 to 0.15625
- routes: int32 [32768, 2], P(('expert', 'dp')), may hold values from 0 to 31, all different within a row; in each aligned block of 128 rows (0 to 127, 128 to 255, ...) at most 10 rows name the same one
- w_in: bfloat16 [64, 1280, 1280], P('expert', None, 'dp'), may hold values from -0.15625 to 0.15625
- w_out: bfloat16 [64, 1280, 1280], P('expert', 'dp'), may hold values from -0.125 to 0.125
- cotangent: bfloat16 [32768, 1280], P(('expert', 'dp')), may hold values from -18 to 18
Outputs:
- input_grad: bfloat16 [32768, 1280], P(('expert', 'dp'))
- grad_in: bfloat16 [64, 1280, 1280], P('expert', None, 'dp')
- grad_out: bfloat16 [64, 1280, 1280], P('expert', 'dp')
- grad_router: float32 [1280, 32], replicated
- grad_gain: float32 [1280], replicated
Inputs may be any that keep to these rules, and one draw needn't show every extreme that they name: `routes`: each row names 2 different experts; among the rows of one device no expert is named more than 10 times.
All inputs are finite; a program needn't handle non-finite values.
Results may differ from a plain program's by a relative error of at most 0.015.
Values may be sent and summed in bfloat16 or wider, within the bound.
A program may use at most 128 MiB of HBM per device.

v0:
```python
import math
import jax
import jax.numpy as jnp
from jax import lax
from jax.sharding import PartitionSpec as P


def gelu_parts(pre):
    coeff = math.sqrt(2.0 / math.pi)
    inner = coeff * (pre + 0.044715 * pre * pre * pre)
    tanh_val = jnp.tanh(inner)
    value = 0.5 * pre * (1.0 + tanh_val)
    slope = 0.5 * (1.0 + tanh_val) + 0.5 * pre * (1.0 - tanh_val * tanh_val) * coeff * (
        1.0 + 3.0 * 0.044715 * pre * pre
    )
    return (value, slope)


def norm_pieces(block, gain):
    values = block.astype(jnp.float32)
    centred_rows = values - jnp.mean(values, axis=1, keepdims=True)
    inverse_deviation = lax.rsqrt(
        jnp.mean(centred_rows * centred_rows, axis=1, keepdims=True) + 1e-06
    )
    normalized_rows = centred_rows * inverse_deviation
    return (
        normalized_rows,
        inverse_deviation,
        (normalized_rows * gain[None, :]).astype(jnp.bfloat16),
    )


def slot_index(routing_rows, expert_list, expert_capacity):
    flat = routing_rows.reshape(-1)
    onehot = (flat[:, None] == jnp.arange(expert_list, dtype=jnp.int32)[None, :]).astype(jnp.int32)
    before = jnp.cumsum(onehot, axis=0) - onehot
    slot = jnp.sum(before * onehot, axis=1)
    return flat * expert_capacity + slot


def expert_pass(rows_m, rows_d, column, w_first, w_second):
    gate = jax.nn.sigmoid(jnp.dot(rows_m, column, preferred_element_type=jnp.float32)[:, 0])
    pre = jnp.dot(rows_m, w_first, preferred_element_type=jnp.float32)
    value, slope = gelu_parts(pre)
    hidden = value.astype(jnp.bfloat16)
    back = jnp.dot(rows_d, w_second.T, preferred_element_type=jnp.float32)
    gate_gradient = jnp.sum(hidden.astype(jnp.float32) * back, axis=1)
    grad_pre = (gate[:, None] * back * slope).astype(jnp.bfloat16)
    grad_y = (gate[:, None] * rows_d.astype(jnp.float32)).astype(jnp.bfloat16)
    grad_second = jnp.dot(hidden.T, grad_y, preferred_element_type=jnp.float32)
    grad_first = jnp.dot(rows_m.T, grad_pre, preferred_element_type=jnp.float32)
    row_gradient = jnp.dot(grad_pre, w_first.T, preferred_element_type=jnp.float32)
    return (row_gradient, gate_gradient, grad_first, grad_second)


def body(prenorm_input, gain, router, routes, w_in, w_out, cotangent):
    halves = lax.axis_size("expert")
    expert_list = halves // 2
    groups = lax.axis_size("dp")
    tok_rows = prenorm_input.shape[0]
    top = routes.shape[1]
    width = prenorm_input.shape[1]
    expert_capacity = max(2, 5 * tok_rows * top // (4 * expert_list))
    slots = expert_list * expert_capacity
    hi = lax.Precision.HIGHEST
    normalized_rows, inverse_deviation, mixed_rows = norm_pieces(prenorm_input, gain)
    where = slot_index(routes, expert_list, expert_capacity)
    places = (where[None, :] == jnp.arange(slots, dtype=jnp.int32)[:, None]).astype(jnp.bfloat16)
    send_m = jnp.dot(
        places, jnp.repeat(mixed_rows, top, axis=0), preferred_element_type=jnp.float32
    ).astype(jnp.bfloat16)
    send_d = jnp.dot(
        places, jnp.repeat(cotangent, top, axis=0), preferred_element_type=jnp.float32
    ).astype(jnp.bfloat16)
    send_m = jnp.repeat(send_m.reshape(expert_list, expert_capacity, width), 2, axis=0)
    send_d = jnp.repeat(send_d.reshape(expert_list, expert_capacity, width), 2, axis=0)
    recv_m, recv_d = (
        lax.all_to_all(send_m, "expert", split_axis=0, concat_axis=0, tiled=True),
        lax.all_to_all(send_d, "expert", split_axis=0, concat_axis=0, tiled=True),
    )
    own = lax.axis_index("expert") // 2
    column = lax.dynamic_slice_in_dim(router, own, 1, 1)
    all_m, all_d = (
        lax.all_gather(recv_m[None], "dp", axis=0, tiled=True),
        lax.all_gather(recv_d[None], "dp", axis=0, tiled=True),
    )
    row_gradient, gate_gradient, grad_first, grad_second = expert_pass(
        all_m.reshape(-1, width), all_d.reshape(-1, width), column, w_in[0], w_out[0]
    )
    summed_rows, summed_gate = (
        lax.psum_scatter(
            row_gradient.reshape(groups, halves * expert_capacity, width).astype(jnp.bfloat16),
            "dp",
            scatter_dimension=0,
            tiled=True,
        ).astype(jnp.float32),
        lax.psum_scatter(
            gate_gradient.reshape(groups, halves * expert_capacity).astype(jnp.bfloat16),
            "dp",
            scatter_dimension=0,
            tiled=True,
        ).astype(jnp.float32),
    )
    back_rows = summed_rows[0].reshape(halves, expert_capacity, width)
    back_gate = summed_gate[0].reshape(halves, expert_capacity)
    grad_in = grad_first[None].astype(jnp.bfloat16)
    grad_out = grad_second[None].astype(jnp.bfloat16)
    ret_rows, ret_gate = (
        lax.all_to_all(
            back_rows.astype(jnp.bfloat16), "expert", split_axis=0, concat_axis=0, tiled=True
        ).astype(back_rows.dtype),
        lax.all_to_all(
            back_gate.astype(jnp.bfloat16), "expert", split_axis=0, concat_axis=0, tiled=True
        ).astype(back_gate.dtype),
    )
    pair_rows = jnp.sum(ret_rows.reshape(expert_list, 2, expert_capacity, width), axis=1).reshape(
        slots, width
    )
    pair_gate = jnp.sum(ret_gate.reshape(expert_list, 2, expert_capacity), axis=1).reshape(slots)
    grad_expert = jnp.sum(jnp.take(pair_rows, where, axis=0).reshape(tok_rows, top, width), axis=1)
    dgate_tok = jnp.take(pair_gate, where, axis=0).reshape(tok_rows, top)
    logits = jnp.dot(mixed_rows, router, preferred_element_type=jnp.float32)
    choose = (routes[:, :, None] == jnp.arange(expert_list, dtype=jnp.int32)[None, None, :]).astype(
        jnp.float32
    )
    gates = jax.nn.sigmoid(jnp.sum(choose * logits[:, None, :], axis=2))
    dlogit = jnp.sum(choose * (dgate_tok * gates * (1.0 - gates))[:, :, None], axis=1)
    mixed_gradient = grad_expert + jnp.dot(dlogit, router.astype(jnp.float32).T, precision=hi)
    router_term = jnp.dot(mixed_rows.astype(jnp.float32).T, dlogit, precision=hi)
    gain_product = jnp.sum(mixed_gradient * normalized_rows, axis=0)
    grad_router, grad_gain = lax.psum((router_term, gain_product), ("expert", "dp"))
    scaled_rows = mixed_gradient * gain[None, :]
    mean_first_term = jnp.mean(scaled_rows, axis=1, keepdims=True)
    mean_second_term = jnp.mean(scaled_rows * normalized_rows, axis=1, keepdims=True)
    norm_backward = inverse_deviation * (
        scaled_rows - mean_first_term - normalized_rows * mean_second_term
    )
    input_grad = (cotangent.astype(jnp.float32) + norm_backward).astype(jnp.bfloat16)
    return (input_grad, grad_in, grad_out, grad_router, grad_gain)


def solution(mesh):
    in_specs = (
        P(("expert", "dp"), None),
        P(),
        P(),
        P(("expert", "dp"), None),
        P("expert", None, "dp"),
        P("expert", "dp", None),
        P(("expert", "dp"), None),
    )
    out_specs = (
        P(("expert", "dp"), None),
        P("expert", None, "dp"),
        P("expert", "dp", None),
        P(),
        P(),
    )
    return jax.shard_map(body, mesh=mesh, in_specs=in_specs, out_specs=out_specs, check_vma=False)
```

profile of v0, /device:TPU:1, one launch (start us, length us, event | category | flops | bytes accessed | tf_op | source)
XLA Modules:
  0.0 642.1 jit_solution(16606466589608056609)
XLA Ops:
  15.1 75.7 %all_to_all.21 = bf16[64,10,1280]{2,1,0:T(8,128)(2,1)S(1)} all-to-all(bf16[64,10,1280]{2,1,0:T(8,128)(2,1)S(1)} %bitcast.60), channel_id=1, replica_groups=mesh['expert'=64,'dp'=4] {'expert'}, dimensions={0} | all-to-all | bytes 3276800 | tf_op jit(solution)/shard_map/all_to_all | solution.py:78
  94.1 68.1 %all_to_all.22 = bf16[64,10,1280]{2,1,0:T(8,128)(2,1)S(1)} all-to-all(bf16[64,10,1280]{2,1,0:T(8,128)(2,1)S(1)} %bitcast.61), channel_id=1, replica_groups=mesh['expert'=64,'dp'=4] {'expert'}, dimensions={0} | all-to-all | bytes 3276800 | tf_op jit(solution)/shard_map/all_to_all | solution.py:79
  163.9 11.2 %copy.54 = bf16[256,10,1280]{2,1,0:T(8,128)(2,1)} copy(bf16[256,10,1280]{2,0,1:T(8,128)(2,1)} %all-gather.5.cloned.1.call-done) | data formatting | bytes 13107200 | tf_op jit(solution)/shard_map/all_gather | solution.py:84
  175.2 13.0 %reshape.183 = bf16[2560,1280]{1,0:T(8,128)(2,1)} reshape(bf16[256,10,1280]{2,1,0:T(8,128)(2,1)} %copy.54) | data formatting | bytes 13107200 | tf_op jit(solution)/shard_map/reshape | solution.py:88
  188.2 4.9 convolution_reduce_fusion
  193.2 4.1 fusion.15
  197.2 34.7 %all-gather.7.cloned.1.call-done = bf16[256,10,1280]{2,0,1:T(8,128)(2,1)} async-done(((bf16[64,10,1280]{2,0,1:T(8,128)(2,1)}), bf16[256,10,1280]{2,0,1:T(8,128)(2,1)}) %all-gather.7.cloned.1.call-update) | async-done | bytes 6553616 | tf_op jit(solution)/shard_map/all_gather | solution.py:85
  231.9 10.8 %copy.56 = bf16[256,10,1280]{2,1,0:T(8,128)(2,1)} copy(bf16[256,10,1280]{2,0,1:T(8,128)(2,1)} %all-gather.7.cloned.1.call-done) | data formatting | bytes 13107200 | tf_op jit(solution)/shard_map/all_gather | solution.py:85
  242.8 12.8 %reshape.188 = bf16[2560,1280]{1,0:T(8,128)(2,1)} reshape(bf16[256,10,1280]{2,1,0:T(8,128)(2,1)} %copy.56) | data formatting | bytes 13107200 | tf_op jit(solution)/shard_map/reshape | solution.py:88
  255.6 8.9 %multiply_reduce_fusion = (bf16[2560]{0:T(1024)(128)(2,1)S(1)}, bf16[2560,320]{0,1:T(8,128)(2,1)S(1)}) fusion(f32[2560,320]{0,1:T(8,128)} %fusion.15, f32[2560]{0:T(1024)S(1)} %add_divide_fusion, bf16[2560,1280]{1,0:T(8,128)(2,1)} %reshape.188, bf16[1,320,1280]{2,1,0:T(8,128)(2,1)S(1)} %copy-done.14), kind=kOutput, calls=%fused_computation.16 | convolution fusion | flops 2117629440 | bytes 12303360 | tf_op jit(solution)/shard_map/dot_general | solution.py:46
  264.6 5.6 convolution_convert_fusion
  271.4 7.0 %all-reduce = bf16[4,640]{1,0:T(4,128)(2,1)S(1)} all-reduce(bf16[4,640]{1,0:T(4,128)(2,1)S(1)} %convert_element_type.107), channel_id=5, replica_groups=mesh['expert'=64,'dp'=4] {'dp'}, use_global_device_ids=true, to_apply=%region_9.10.clone | all-reduce | flops 2560 | bytes 10240
  279.9 13.2 %all-to-all-start.3 = ((bf16[64,1,10]{2,1,0:T(2,128)(2,1)}), bf16[64,1,10]{2,1,0:T(2,128)(2,1)S(1)}, u32[]{:S(2)}, u32[]{:S(2)}) async-start(bf16[64,1,10]{2,1,0:T(2,128)(2,1)} %convert_element_type.119), calls=%async_computation.4 | async-start | bytes 65536 | tf_op jit(solution)/shard_map/all_to_all | solution.py:112
  293.1 46.7 %reduce-scatter.2.cloned.1.call-done = bf16[1,640,1280]{2,1,0:T(8,128)(2,1)} async-done(((bf16[4,640,1280]{2,1,0:T(8,128)(2,1)}), bf16[1,640,1280]{2,1,0:T(8,128)(2,1)}) %reduce-scatter.2.cloned.1.call-update) | async-done | bytes 1638416 | tf_op jit(solution)/shard_map/reduce_scatter | solution.py:91
  339.8 4.0 convert_element_type.103
  344.4 10.7 %all-to-all-start.2 = ((bf16[64,10,1280]{2,1,0:T(8,128)(2,1)}), bf16[64,10,1280]{2,1,0:T(8,128)(2,1)S(1)}, u32[]{:S(2)}, u32[]{:S(2)}) async-start(bf16[64,10,1280]{2,1,0:T(8,128)(2,1)} %convert_element_type.103), calls=%async_computation.3 | async-start | bytes 5242880 | tf_op jit(solution)/shard_map/all_to_all | solution.py:109
  360.9 6.7 %fusion.10 = bf16[1,1280,320]{1,2,0:T(8,128)(2,1)} fusion(bf16[2560,320]{0,1:T(8,128)(2,1)} %copy-done.15, bf16[2560,1280]{1,0:T(8,128)(2,1)} %reshape.183), kind=kOutput, calls=%fused_computation.22 | convolution fusion | flops 2097561600 | bytes 9011200 | tf_op jit(solution)/shard_map/dot_general | solution.py:51
  367.6 6.9 %fusion.11 = bf16[1,320,1280]{2,1,0:T(8,128)(2,1)} fusion(bf16[2560,1280]{1,0:T(8,128)(2,1)} %reshape.188, f32[2560]{0:T(1024)S(1)} %add_divide_fusion, f32[2560,320]{0,1:T(8,128)S(1)} %copy-done.17), kind=kOutput, calls=%fused_computation.23 | convolution fusion | flops 2114764800 | bytes 10659840 | tf_op jit(solution)/shard_map/dot_general | solution.py:50
  376.1 2.2 gather_fusion.1
  384.6 31.6 %all-to-all-done.2 = bf16[64,10,1280]{2,1,0:T(8,128)(2,1)S(1)} async-done(((bf16[64,10,1280]{2,1,0:T(8,128)(2,1)}), bf16[64,10,1280]{2,1,0:T(8,128)(2,1)S(1)}, u32[]{:S(2)}, u32[]{:S(2)}) %all-to-all-start.2) | async-done | bytes 1638432 | tf_op jit(solution)/shard_map/all_to_all | solution.py:109
  420.1 2.2 gather_fusion
  422.3 2.1 gather.13
  428.0 75.6 %psum.15 = f32[1280]{0:T(1024)} all-reduce(f32[1280]{0:T(1024)S(1)} %get-tuple-element.5), channel_id=1, replica_groups=mesh['expert'=64,'dp'=4] {'expert','dp'}, use_global_device_ids=true, to_apply=%region_17.18 | all-reduce | flops 1280 | bytes 10240 | tf_op jit(solution)/shard_map/psum | solution.py:131
  503.6 130.3 %all-reduce.3.cloned.1.call-done = f32[1280,32]{0,1:T(8,128)} async-done(((f32[1280,32]{0,1:T(8,128)}), f32[1280,32]{0,1:T(8,128)}) %all-reduce.3.cloned.1.call-update) | async-done | bytes 163856 | tf_op jit(solution)/shard_map/psum | solution.py:131
  (103 shorter events, 38.7 us)
Async XLA Ops:
  7.2 186.0 %copy-start = (bf16[1,1280,320]{1,2,0:T(8,128)(2,1)S(1)}, bf16[1,1280,320]{1,2,0:T(8,128)(2,1)}, u32[]{:S(2)}) copy-start(bf16[1,1280,320]{1,2,0:T(8,128)(2,1)} %param.11) | copy-start | bytes 2457604
  7.2 156.7 %all-gather.5.cloned.1.call-start = ((), (), s32[]{:S(2)}) async-start(), calls=%async_computation.7 | async-start | bytes 8192000 | tf_op jit(solution)/shard_map/all_gather | solution.py:84
  11.6 3.3 copy-start.12
  12.9 0.7 copy-start.3
  90.8 1.7 copy-start.4
  92.5 139.5 %all-gather.7.cloned.1.call-start = ((), (), s32[]{:S(2)}) async-start(), calls=%async_computation.8 | async-start | bytes 8192000 | tf_op jit(solution)/shard_map/all_gather | solution.py:85
  163.8 176.0 %reduce-scatter.2.cloned.1.call-start = ((), (), s32[]{:S(2)}) async-start(), calls=%async_computation.5 | async-start | bytes 8192000 | tf_op jit(solution)/shard_map/reduce_scatter | solution.py:91
  175.2 13.0 %copy-start.6 = (bf16[1280,32]{0,1:T(8,128)(2,1)S(1)}, bf16[1280,32]{0,1:T(8,128)(2,1)}, u32[]{:S(2)}) copy-start(bf16[1280,32]{0,1:T(8,128)(2,1)} %param.9) | copy-start | bytes 245764
  188.2 5.0 copy-start.1
  242.8 12.8 %copy-start.14 = (bf16[1,320,1280]{2,1,0:T(8,128)(2,1)S(1)}, bf16[1,320,1280]{2,1,0:T(8,128)(2,1)}, u32[]{:S(2)}) copy-start(bf16[1,320,1280]{2,1,0:T(8,128)(2,1)} %param.12) | copy-start | bytes 2457604
  264.6 5.6 copy-start.15
  270.1 0.7 copy-start.16
  279.9 63.9 %all-to-all-start.3 = ((bf16[64,1,10]{2,1,0:T(2,128)(2,1)}), bf16[64,1,10]{2,1,0:T(2,128)(2,1)S(1)}, u32[]{:S(2)}, u32[]{:S(2)}) async-start(bf16[64,1,10]{2,1,0:T(2,128)(2,1)} %convert_element_type.119), calls=%async_computation.4 | async-start | bytes 65536 | tf_op jit(solution)/shard_map/all_to_all | solution.py:112
  343.8 12.2 %copy-start.11 = (s32[128,2]{0,1:T(2,128)S(1)}, s32[128,2]{0,1:T(2,128)}, u32[]{:S(2)}) copy-start(s32[128,2]{0,1:T(2,128)} %param.10) | copy-start | bytes 3076
  343.8 0.6 copy-start.7
  344.4 71.8 %all-to-all-start.2 = ((bf16[64,10,1280]{2,1,0:T(8,128)(2,1)}), bf16[64,10,1280]{2,1,0:T(8,128)(2,1)S(1)}, u32[]{:S(2)}, u32[]{:S(2)}) async-start(bf16[64,10,1280]{2,1,0:T(8,128)(2,1)} %convert_element_type.103), calls=%async_computation.3 | async-start | bytes 5242880 | tf_op jit(solution)/shard_map/all_to_all | solution.py:109
  355.1 278.8 %all-reduce.3.cloned.1.call-start = ((), (), s32[]{:S(2)}) async-start(), calls=%async_computation.6 | async-start | bytes 327680 | tf_op jit(solution)/shard_map/psum | solution.py:131
  360.9 6.7 %copy-start.17 = (f32[2560,320]{0,1:T(8,128)S(1)}, f32[2560,320]{0,1:T(8,128)}, u32[]{:S(2)}) copy-start(f32[2560,320]{0,1:T(8,128)} %fusion.15) | copy-start | bytes 9830404
  367.6 6.9 %copy-start.8 = (bf16[64,1,10]{2,1,0:T(2,128)(2,1)S(1)}, bf16[64,1,10]{2,1,0:T(2,128)(2,1)}, u32[]{:S(2)}) copy-start(bf16[64,1,10]{2,1,0:T(2,128)(2,1)} %copy-done.7) | copy-start | bytes 3844
  420.1 4.4 copy-start.10
  422.3 3.9 copy-start.2
  422.3 3.9 copy-start.9
  422.3 3.9 copy-start.13
  422.3 4.6 copy-start.5
Sparse Core Ops, SparseCore 0:
  92.6 66.4 all-gather.4
  164.0 67.9 all-gather.6
  270.3 69.4 reduce-scatter.1
  384.7 249.2 all-reduce.2
where the time goes:
time: 644 us; the launch traced here: 642 us
  waiting for transfers between devices  243 us (38%)
  blocking collectives  226 us (35%)
  local copies, waits for them, and re-layouts  79.3 us (12%)
  matrix products  41.6 us (6%)
  starting transfers between devices  24.1 us (4%)
  between operations  14.1 us (2%)
  other arithmetic  13.1 us (2%)
    psum x1, waiting for transfers between devices, body(): lax.psum((router_term, gain_product), ('expert', 'dp'))  130 us
    all_to_all x1, blocking collectives, body(): lax.all_to_all(send_m, 'expert', split_axis=0, concat_axis=0, tiled=True)  75.7 us
    psum x1, blocking collectives, body(): lax.psum((router_term, gain_product), ('expert', 'dp'))  75.6 us
    all_to_all x1, blocking collectives, body(): lax.all_to_all(send_d, 'expert', split_axis=0, concat_axis=0, tiled=True)  68.1 us
    reduce_scatter x1, waiting for transfers between devices, body(): lax.psum_scatter(row_gradient.reshape(groups, halves * expert_capacity, w...  46.7 us
    all_gather x1, waiting for transfers between devices, body(): lax.all_gather(recv_d[None], 'dp', axis=0, tiled=True)  34.7 us
    all_to_all x1, waiting for transfers between devices, body(): lax.all_to_all(back_rows.astype(jnp.bfloat16), 'expert', split_axis=0, co...  31.6 us
    all_to_all x1, starting transfers between devices, body(): lax.all_to_all(back_gate.astype(jnp.bfloat16), 'expert', split_axis=0, co...  13.2 us
  transfers between devices with their start and end apart: 6, of which 4 were waited for; matrix products, arithmetic and copies ran while one was open for 13% of the time, Pallas kernels for 0%

commit v1 on v0

--- a/solution.py
+++ b/solution.py
@@ -1,8 +1,40 @@
+import functools
 import math
 import jax
 import jax.numpy as jnp
 from jax import lax
 from jax.sharding import PartitionSpec as P
+
+
+def ratios_mix(message, pos_dim):
+    seen_now, part_now, last = (lax.axis_size("dp"), lax.axis_index("dp"), message.shape[pos_dim])
+    store = [d * seen_now if num == pos_dim else d for num, d in enumerate(message.shape)]
+    out_arr = lax.dynamic_update_slice_in_dim(
+        jnp.zeros(store, message.dtype), message, part_now * last, axis=pos_dim
+    )
+    extra = passed = message
+    for dev in range(1, seen_now // 2 + 1):
+        extra = lax.ppermute(
+            extra,
+            axis_name="dp",
+            perm=list(map(lambda num: (num, (num + 1) % seen_now), range(seen_now))),
+        )
+        out_arr = lax.dynamic_update_slice_in_dim(
+            out_arr, extra, (part_now - dev) % seen_now * last, axis=pos_dim
+        )
+        if 2 * dev < seen_now:
+            passed = lax.ppermute(
+                passed,
+                axis_name="dp",
+                perm=list(map(lambda num: (num, (num - 1) % seen_now), range(seen_now))),
+            )
+            out_arr = lax.dynamic_update_slice_in_dim(
+                out_arr, passed, (part_now + dev) % seen_now * last, axis=pos_dim
+            )
+    return out_arr
+
+
+watch_the_slot = functools.partial(ratios_mix, pos_dim=0)
 
 
 def gelu_parts(pre):
@@ -82,7 +114,7 @@
     column = lax.dynamic_slice_in_dim(router, own, 1, 1)
     all_m, all_d = (
         lax.all_gather(recv_m[None], "dp", axis=0, tiled=True),
-        lax.all_gather(recv_d[None], "dp", axis=0, tiled=True),
+        watch_the_slot(recv_d[None]),
     )
     row_gradient, gate_gradient, grad_first, grad_second = expert_pass(
         all_m.reshape(-1, width), all_d.reshape(-1, width), column, w_in[0], w_out[0]

time: 644 us -> 683 us (1.061)
  waiting for transfers between devices: 243 us -> 268 us
  starting transfers between devices: 24.1 us -> 33.4 us
  matrix products: 41.6 us -> 34.7 us
    ppermute x0 -> x3, waiting for transfers between devices: none -> 59.2 us  [the longest x2 59.2 us: ratios_mix(): lax.ppermute(extra, axis_name='dp', perm=list(map(lambda num: (num, (num...]
    all_gather x1 -> x0, waiting for transfers between devices: 34.7 us -> none  [body(): lax.all_gather(recv_d[None], 'dp', axis=0, tiled=True)]
    ppermute x0 -> x3, starting transfers between devices: none -> 13.6 us  [the longest x2 12.2 us: ratios_mix(): lax.ppermute(extra, axis_name='dp', perm=list(map(lambda num: (num, (num...]
    dynamic_update_slice x0 -> x4, local copies, waits for them, and re-layouts: none -> 12 us  [the longest x2 6.38 us: ratios_mix(): lax.dynamic_update_slice_in_dim(out_arr, extra, (part_now - dev) % seen_n...]
    all_gather x1 -> x0, local copies, waits for them, and re-layouts: 10.8 us -> none  [body(): lax.all_gather(recv_d[None], 'dp', axis=0, tiled=True)]
  transfers between devices with their start and end apart: 6 -> 8, of which waited for: 4 -> 5; matrix products, arithmetic and copies ran while one was open for 13% -> 12% of each run, Pallas kernels for 0% -> 0%
where the time goes in v1:
time: 683 us; the launch traced here: 675 us
  waiting for transfers between devices  268 us (39%)
  blocking collectives  225 us (33%)
  local copies, waits for them, and re-layouts  85.6 us (13%)
  matrix products  34.7 us (5%)
  starting transfers between devices  33.4 us (5%)
  between operations  14.6 us (2%)
  other arithmetic  13.2 us (2%)
    psum x1, waiting for transfers between devices, body(): lax.psum((router_term, gain_product), ('expert', 'dp'))  131 us
    all_to_all x1, blocking collectives, body(): lax.all_to_all(send_m, 'expert', split_axis=0, concat_axis=0, tiled=True)  75.7 us
    psum x1, blocking collectives, body(): lax.psum((router_term, gain_product), ('expert', 'dp'))  75.4 us
    all_to_all x1, blocking collectives, body(): lax.all_to_all(send_d, 'expert', split_axis=0, concat_axis=0, tiled=True)  68.1 us
    ppermute x2, waiting for transfers between devices, ratios_mix(): lax.ppermute(extra, axis_name='dp', perm=list(map(lambda num: (num, (num...  59.2 us
    reduce_scatter x1, waiting for transfers between devices, body(): lax.psum_scatter(row_gradient.reshape(groups, halves * expert_capacity, w...  46.5 us
    all_to_all x1, waiting for transfers between devices, body(): lax.all_to_all(back_rows.astype(jnp.bfloat16), 'expert', split_axis=0, co...  31.8 us
  transfers between devices with their start and end apart: 8, of which 5 were waited for; matrix products, arithmetic and copies ran while one was open for 12% of the time, Pallas kernels for 0%

profile of v1, /device:TPU:1, one launch (start us, length us, event | category | flops | bytes accessed | tf_op | source)
XLA Modules:
  0.0 674.9 jit_solution(5699666792328404677)
XLA Ops:
  15.1 75.7 %all_to_all.21 = bf16[64,10,1280]{2,1,0:T(8,128)(2,1)S(1)} all-to-all(bf16[64,10,1280]{2,1,0:T(8,128)(2,1)S(1)} %bitcast.63), channel_id=1, replica_groups=mesh['expert'=64,'dp'=4] {'expert'}, dimensions={0} | all-to-all | bytes 3276800 | tf_op jit(solution)/shard_map/all_to_all | solution.py:110
  94.1 68.1 %all_to_all.22 = bf16[64,10,1280]{2,1,0:T(8,128)(2,1)S(1)} all-to-all(bf16[64,10,1280]{2,1,0:T(8,128)(2,1)S(1)} %bitcast.64), channel_id=1, replica_groups=mesh['expert'=64,'dp'=4] {'expert'}, dimensions={0} | all-to-all | bytes 3276800 | tf_op jit(solution)/shard_map/all_to_all | solution.py:111
  166.5 35.9 %collective-permute-done = bf16[1,64,10,1280]{3,1,2,0:T(8,128)(2,1)} collective-permute-done((bf16[1,64,10,1280]{3,1,2,0:T(8,128)(2,1)}, bf16[1,64,10,1280]{3,1,2,0:T(8,128)(2,1)}, u32[]{:S(2)}, u32[]{:S(2)}) %collective-permute-start) | collective-permute-done | bytes 1638432 | tf_op jit(solution)/shard_map/ppermute | solution.py:17
  202.4 11.0 %collective-permute-start.2 = (bf16[1,64,10,1280]{3,1,2,0:T(8,128)(2,1)}, bf16[1,64,10,1280]{3,1,2,0:T(8,128)(2,1)S(1)}, u32[]{:S(2)}, u32[]{:S(2)}) collective-permute-start(bf16[1,64,10,1280]{3,1,2,0:T(8,128)(2,1)} %collective-permute-done), channel_id=1, source_target_pairs={{0,1},{1,2},{2,3},{3,0},{4,5},{5,6},{6,7},{7,4},{8,9},{9,10},{10,1... | collective-permute-start | bytes 4915208 | tf_op jit(solution)/shard_map/ppermute | solution.py:17
  213.4 4.8 broadcast_in_dim.58
  219.9 3.9 copy_dynamic-update-slice_fusion.2
  223.8 3.9 copy_dynamic-update-slice_fusion.1
  227.7 23.3 %collective-permute-done.2 = bf16[1,64,10,1280]{3,1,2,0:T(8,128)(2,1)S(1)} collective-permute-done((bf16[1,64,10,1280]{3,1,2,0:T(8,128)(2,1)}, bf16[1,64,10,1280]{3,1,2,0:T(8,128)(2,1)S(1)}, u32[]{:S(2)}, u32[]{:S(2)}) %collective-permute-start.2) | collective-permute-done | bytes 1638432 | tf_op jit(solution)/shard_map/ppermute | solution.py:17
  253.4 12.8 %reshape.188 = bf16[2560,1280]{1,0:T(8,128)(2,1)} reshape(bf16[4,64,10,1280]{3,2,1,0:T(8,128)(2,1)} %copy_dynamic-update-slice_fusion) | data formatting | bytes 13107200 | tf_op jit(solution)/shard_map/reshape | solution.py:120
  266.2 10.8 %copy.60 = bf16[256,10,1280]{2,1,0:T(8,128)(2,1)} copy(bf16[256,10,1280]{2,0,1:T(8,128)(2,1)} %all-gather.3.cloned.1.call-done) | data formatting | bytes 13107200 | tf_op jit(solution)/shard_map/all_gather | solution.py:116
  277.0 12.8 %reshape.183 = bf16[2560,1280]{1,0:T(8,128)(2,1)} reshape(bf16[256,10,1280]{2,1,0:T(8,128)(2,1)} %copy.60) | data formatting | bytes 13107200 | tf_op jit(solution)/shard_map/reshape | solution.py:120
  289.9 4.8 convolution_reduce_fusion
  297.1 4.0 multiply_reduce_fusion
  302.3 5.5 convolution_convert_fusion
  309.1 6.2 all-reduce
  316.7 8.8 %all-to-all-start.3 = ((bf16[64,1,10]{2,1,0:T(2,128)(2,1)}), bf16[64,1,10]{2,1,0:T(2,128)(2,1)S(1)}, u32[]{:S(2)}, u32[]{:S(2)}) async-start(bf16[64,1,10]{2,1,0:T(2,128)(2,1)} %convert_element_type.119), calls=%async_computation.4 | async-start | bytes 65536 | tf_op jit(solution)/shard_map/all_to_all | solution.py:144
  325.6 46.5 %reduce-scatter.2.cloned.1.call-done = bf16[1,640,1280]{2,1,0:T(8,128)(2,1)} async-done(((bf16[4,640,1280]{2,1,0:T(8,128)(2,1)}), bf16[1,640,1280]{2,1,0:T(8,128)(2,1)}) %reduce-scatter.2.cloned.1.call-update) | async-done | bytes 1638416 | tf_op jit(solution)/shard_map/reduce_scatter | solution.py:123
  372.0 4.0 convert_element_type.103
  376.6 10.8 %all-to-all-start.2 = ((bf16[64,10,1280]{2,1,0:T(8,128)(2,1)}), bf16[64,10,1280]{2,1,0:T(8,128)(2,1)S(1)}, u32[]{:S(2)}, u32[]{:S(2)}) async-start(bf16[64,10,1280]{2,1,0:T(8,128)(2,1)} %convert_element_type.103), calls=%async_computation.3 | async-start | bytes 5242880 | tf_op jit(solution)/shard_map/all_to_all | solution.py:141
  393.3 6.7 fusion.10
  400.0 6.9 %fusion.11 = bf16[1,320,1280]{2,1,0:T(8,128)(2,1)} fusion(bf16[2560,1280]{1,0:T(8,128)(2,1)} %reshape.188, f32[2560]{0:T(1024)S(1)} %add_divide_fusion, f32[2560,320]{0,1:T(8,128)S(1)} %copy-done.18), kind=kOutput, calls=%fused_computation.26 | convolution fusion | flops 2114764800 | bytes 10659840 | tf_op jit(solution)/shard_map/dot_general | solution.py:82
  416.7 31.8 %all-to-all-done.2 = bf16[64,10,1280]{2,1,0:T(8,128)(2,1)S(1)} async-done(((bf16[64,10,1280]{2,1,0:T(8,128)(2,1)}), bf16[64,10,1280]{2,1,0:T(8,128)(2,1)S(1)}, u32[]{:S(2)}, u32[]{:S(2)}) %all-to-all-start.2) | async-done | bytes 1638432 | tf_op jit(solution)/shard_map/all_to_all | solution.py:141
  460.3 75.4 %psum.15 = f32[1280]{0:T(1024)} all-reduce(f32[1280]{0:T(1024)S(1)} %get-tuple-element.5), channel_id=1, replica_groups=mesh['expert'=64,'dp'=4] {'expert','dp'}, use_global_device_ids=true, to_apply=%region_17.18 | all-reduce | flops 1280 | bytes 10240 | tf_op jit(solution)/shard_map/psum | solution.py:163
  535.7 130.7 %all-reduce.3.cloned.1.call-done = f32[1280,32]{0,1:T(8,128)} async-done(((f32[1280,32]{0,1:T(8,128)}), f32[1280,32]{0,1:T(8,128)}) %all-reduce.3.cloned.1.call-update) | async-done | bytes 163856 | tf_op jit(solution)/shard_map/psum | solution.py:163
  (117 shorter events, 55.4 us)
Async XLA Ops:
  7.2 287.6 %copy-start = (bf16[1,1280,320]{1,2,0:T(8,128)(2,1)S(1)}, bf16[1,1280,320]{1,2,0:T(8,128)(2,1)}, u32[]{:S(2)}) copy-start(bf16[1,1280,320]{1,2,0:T(8,128)(2,1)} %param.11) | copy-start | bytes 2457604
  7.2 259.0 %all-gather.3.cloned.1.call-start = ((), (), s32[]{:S(2)}) async-start(), calls=%async_computation.7 | async-start | bytes 8192000 | tf_op jit(solution)/shard_map/all_gather | solution.py:116
  11.6 3.3 copy-start.12
  92.5 279.6 %reduce-scatter.2.cloned.1.call-start = ((), (), s32[]{:S(2)}) async-start(), calls=%async_computation.5 | async-start | bytes 8192000 | tf_op jit(solution)/shard_map/reduce_scatter | solution.py:123
  163.8 38.6 %collective-permute-start = (bf16[1,64,10,1280]{3,1,2,0:T(8,128)(2,1)}, bf16[1,64,10,1280]{3,1,2,0:T(8,128)(2,1)}, u32[]{:S(2)}, u32[]{:S(2)}) collective-permute-start(bf16[1,64,10,1280]{3,1,2,0:T(8,128)(2,1)} %copy.61), channel_id=1, source_target_pairs={{0,1},{1,2},{2,3},{3,0},{4,5},{5,6},{6,7},{7,4},{8,9},{9,10},{10,1... | collective-permute-start | bytes 4915208 | tf_op jit(solution)/shard_map/ppermute | solution.py:17
  165.0 58.8 %collective-permute-start.1 = (bf16[1,64,10,1280]{3,1,2,0:T(8,128)(2,1)}, bf16[1,64,10,1280]{3,1,2,0:T(8,128)(2,1)}, u32[]{:S(2)}, u32[]{:S(2)}) collective-permute-start(bf16[1,64,10,1280]{3,1,2,0:T(8,128)(2,1)} %copy.61), channel_id=1, source_target_pairs={{0,3},{1,0},{2,1},{3,2},{4,7},{5,4},{6,5},{7,6},{8,11},{9,8},{10,9... | collective-permute-start | bytes 4915208 | tf_op jit(solution)/shard_map/ppermute | solution.py:26
  202.4 48.6 %collective-permute-start.2 = (bf16[1,64,10,1280]{3,1,2,0:T(8,128)(2,1)}, bf16[1,64,10,1280]{3,1,2,0:T(8,128)(2,1)S(1)}, u32[]{:S(2)}, u32[]{:S(2)}) collective-permute-start(bf16[1,64,10,1280]{3,1,2,0:T(8,128)(2,1)} %collective-permute-done), channel_id=1, source_target_pairs={{0,1},{1,2},{2,3},{3,0},{4,5},{5,6},{6,7},{7,4},{8,9},{9,10},{10,1... | collective-permute-start | bytes 4915208 | tf_op jit(solution)/shard_map/ppermute | solution.py:17
  277.0 12.8 %copy-start.6 = (bf16[1280,32]{0,1:T(8,128)(2,1)S(1)}, bf16[1280,32]{0,1:T(8,128)(2,1)}, u32[]{:S(2)}) copy-start(bf16[1280,32]{0,1:T(8,128)(2,1)} %param.9) | copy-start | bytes 245764
  289.9 4.9 copy-start.1
  289.9 7.2 %slice-start = ((s8[6553600]{0:T(1024)(128)(4,1)}), s8[4194304]{0:T(1024)(128)(4,1)S(1)}, s32[]{:S(2)}) async-start(s8[6553600]{0:T(1024)(128)(4,1)} %bitcast.65), calls=%async_computation.8 | async-start | bytes 8388608
  294.7 2.4 slice-start.1
  294.8 2.4 copy-start.14
  297.1 4.0 copy-start.17
  316.7 59.3 %all-to-all-start.3 = ((bf16[64,1,10]{2,1,0:T(2,128)(2,1)}), bf16[64,1,10]{2,1,0:T(2,128)(2,1)S(1)}, u32[]{:S(2)}, u32[]{:S(2)}) async-start(bf16[64,1,10]{2,1,0:T(2,128)(2,1)} %convert_element_type.119), calls=%async_computation.4 | async-start | bytes 65536 | tf_op jit(solution)/shard_map/all_to_all | solution.py:144
  376.0 12.3 %copy-start.11 = (s32[128,2]{0,1:T(2,128)S(1)}, s32[128,2]{0,1:T(2,128)}, u32[]{:S(2)}) copy-start(s32[128,2]{0,1:T(2,128)} %param.10) | copy-start | bytes 3076
  376.6 71.9 %all-to-all-start.2 = ((bf16[64,10,1280]{2,1,0:T(8,128)(2,1)}), bf16[64,10,1280]{2,1,0:T(8,128)(2,1)S(1)}, u32[]{:S(2)}, u32[]{:S(2)}) async-start(bf16[64,10,1280]{2,1,0:T(8,128)(2,1)} %convert_element_type.103), calls=%async_computation.3 | async-start | bytes 5242880 | tf_op jit(solution)/shard_map/all_to_all | solution.py:141
  387.5 279.0 %all-reduce.3.cloned.1.call-start = ((), (), s32[]{:S(2)}) async-start(), calls=%async_computation.6 | async-start | bytes 327680 | tf_op jit(solution)/shard_map/psum | solution.py:163
  393.3 6.7 copy-start.18
  400.0 6.9 %copy-start.8 = (bf16[64,1,10]{2,1,0:T(2,128)(2,1)S(1)}, bf16[64,1,10]{2,1,0:T(2,128)(2,1)}, u32[]{:S(2)}) copy-start(bf16[64,1,10]{2,1,0:T(2,128)(2,1)} %copy-done.7) | copy-start | bytes 3844
  452.4 4.4 copy-start.10
  454.6 3.9 copy-start.2
  454.6 3.9 copy-start.9
  454.6 3.9 copy-start.13
  454.6 4.6 copy-start.5
  (5 other events, 4.9 us)
Sparse Core Ops, SparseCore 0:
  92.6 66.4 all-gather.2
  308.0 64.0 reduce-scatter.1
  416.9 249.5 all-reduce.2
